TPU v7x, 32 devices: a whole 2x2x4 slice. The times are simulated.
32 devices in a mesh: grp: 8 (over z, x), dev: 4 (over y, core).
Axes of the slice: x: 2, y: 2, z: 4, core: 2. Of those that a mesh axis runs over, the one named last changes fastest.
Arguments:
- block_states: float32 [256, 5, 4096], P(('grp', 'dev')), may hold values from -2 to 10.5, as said below
- dest_dev: int32 [256], P('grp'), may hold values from -1 to 3, as said below
- dest_slot: int32 [256], P('grp'), may hold values from 0 to 3, as said below
- neighbours: int32 [2, 128], P(None, 'grp'), may hold values from -1 to 15, as said below
- coarse_map: int32 [4, 32], P('dev'), may hold values from 0 to 31, each once within a row
Outputs:
- advanced: float32 [128, 5, 4096], P(('grp', 'dev'))
- registers: float32 [32, 5, 256], P(('grp', 'dev'))
Inputs may be any that keep to these rules, and one draw needn't show every extreme that they name: `block_states`: every slot holds a physical state: density 0.5 to 2, each velocity component -1 to 1, pressure 0.3 to 3. `dest_dev`: each pair of a receiving device index and a slot 0 .. 3 of a group gets exactly one patch; a device keeps its own patches or sends at most one patch to each of the next 3 device indices of its group (counted modulo 4) and to no other. `dest_slot`: see dest_dev. Index dev * 4 + slot within the group; neighbours are mutual (neighbours[1, a] = b exactly when neighbours[0, b] = a, within a group), a neighbour's index differs from the patch's own by at most 3, and -1 marks a domain boundary. `coarse_map`: for each device index a permutation: value m names register m // 4 in the group order, quadrant m % 4.
All inputs are finite; a program needn't handle non-finite values.
Results may differ from a plain program's by a relative error of at most 0.0003.
Values sent between devices are 32-bit elements; how exact they have to be, the bound alone decides.
No kernel may reach another device: no remote copies, remote signals or barrier semaphores. Data moves between devices by JAX's collectives and lax.ppermute only.
A program may use at most 64 MiB of HBM per device.

v0:
```python
import jax
import jax.numpy as jnp
from jax import lax
from jax.sharding import PartitionSpec as P

SIDE_LENGTH = 16
DEVICE_PATCHES = 4
P_DEV = 8
GAMMA = 1.4
COURANT = 0.2


def passed_along(block, axis, distance):
    devices = range(lax.axis_size(axis))
    route = [((i - distance) % len(devices), i) for i in devices]
    return lax.ppermute(block, axis, route)


def shifted(shard, axis, by):
    size = lax.axis_size(axis)
    pairs = [(i, i + by) for i in range(size) if 0 <= i + by < size]
    return lax.ppermute(shard, axis, pairs)


def primitives(conserved):
    density = conserved[..., 0, :, :]
    inverse = 1.0 / density
    vel_x = conserved[..., 1, :, :] * inverse
    vel_y = conserved[..., 2, :, :] * inverse
    vel_z = conserved[..., 3, :, :] * inverse
    kinetic = 0.5 * (
        conserved[..., 1, :, :] * vel_x
        + conserved[..., 2, :, :] * vel_y
        + conserved[..., 3, :, :] * vel_z
    )
    pressure = (GAMMA - 1.0) * (conserved[..., 4, :, :] - kinetic)
    return jnp.stack([density, vel_x, vel_y, vel_z, pressure], axis=-3)


def euler_flux(primitive):
    density = primitive[..., 0, :, :]
    vel_x = primitive[..., 1, :, :]
    vel_y = primitive[..., 2, :, :]
    vel_z = primitive[..., 3, :, :]
    pressure = primitive[..., 4, :, :]
    mass_flux = density * vel_x
    energy = pressure / (GAMMA - 1.0) + 0.5 * density * (
        vel_x * vel_x + vel_y * vel_y + vel_z * vel_z
    )
    fluxes = jnp.stack(
        [
            mass_flux,
            mass_flux * vel_x + pressure,
            mass_flux * vel_y,
            mass_flux * vel_z,
            vel_x * (energy + pressure),
        ],
        axis=-3,
    )
    conserved = jnp.stack([density, mass_flux, density * vel_y, density * vel_z, energy], axis=-3)
    speeds = jnp.abs(vel_x) + jnp.sqrt(GAMMA * pressure / density)
    return (fluxes, conserved, speeds)


def advance(block_volumes, lower_ghost, upper_ghost):
    extended = jnp.concatenate([lower_ghost, block_volumes, upper_ghost], axis=-2)
    primitive = primitives(extended)
    below_diff = primitive[..., 1:-1, :] - primitive[..., :-2, :]
    above_diff = primitive[..., 2:, :] - primitive[..., 1:-1, :]
    slopes = (
        0.5
        * (jnp.sign(below_diff) + jnp.sign(above_diff))
        * jnp.minimum(jnp.abs(below_diff), jnp.abs(above_diff))
    )
    centre = primitive[..., 1:-1, :]
    left_state = (centre + 0.5 * slopes)[..., :-1, :]
    right_state = (centre - 0.5 * slopes)[..., 1:, :]
    left_flux, left_cons, left_speed = euler_flux(left_state)
    right_flux, right_cons, right_speed = euler_flux(right_state)
    largest = jnp.maximum(left_speed, right_speed)[..., None, :, :]
    interface = 0.5 * (left_flux + right_flux) - 0.5 * largest * (right_cons - left_cons)
    updated = block_volumes - COURANT * (interface[..., 1:, :] - interface[..., :-1, :])
    return (updated, interface[..., -1, :])


def fill_edges(block_volumes, lower_ghost, upper_ghost, lower_nbr, upper_nbr):
    first = block_volumes[:, :, :1, :]
    last = block_volumes[:, :, -1:, :]
    lower_ghost = jnp.where(
        (lower_nbr < 0)[:, None, None, None], jnp.concatenate([first, first], axis=2), lower_ghost
    )
    upper_ghost = jnp.where(
        (upper_nbr < 0)[:, None, None, None], jnp.concatenate([last, last], axis=2), upper_ghost
    )
    return (lower_ghost, upper_ghost)


def coarsen(interface):
    half_edge = SIDE_LENGTH // 2
    shaped = interface.reshape(interface.shape[:-1] + (half_edge, 2, half_edge, 2))
    return shaped.mean(axis=(-3, -1))


def spread(coarse, quadrant):
    half_edge = SIDE_LENGTH // 2
    tiled = jnp.tile(coarse, (1,) * (coarse.ndim - 2) + (2, 2))
    row_ids = jnp.arange(SIDE_LENGTH, dtype=jnp.int32) // half_edge
    inside = (row_ids[:, None] == (quadrant // 2)[..., None, None]) & (
        row_ids[None, :] == (quadrant % 2)[..., None, None]
    )
    placed = tiled * inside.astype(tiled.dtype)[..., None, :, :]
    return placed.reshape(placed.shape[:-2] + (SIDE_LENGTH * SIDE_LENGTH,))


def selected_lines(weights, operand):
    flat = operand.reshape(operand.shape[0], -1)
    picked = jnp.dot(weights, flat, precision=lax.Precision.HIGHEST)
    return picked.reshape((weights.shape[0],) + operand.shape[1:])


def add_faces(totals, arrived, labels, lower_nbr, upper_nbr):
    below_sel = (lower_nbr[:, None] == labels[None, :]).astype(jnp.float32)
    above_sel = (upper_nbr[:, None] == labels[None, :]).astype(jnp.float32)
    return (
        totals[0] + selected_lines(below_sel, arrived[0]),
        totals[1] + selected_lines(above_sel, arrived[1]),
    )


def landing_rows(plan_dev, plan_slot, source_dev, my_dev, wanted):
    from_dev = lax.dynamic_index_in_dim(plan_dev, source_dev, 0, keepdims=False)
    from_slot = lax.dynamic_index_in_dim(plan_slot, source_dev, 0, keepdims=False)
    hits = (from_dev[None, :] == my_dev) & (from_slot[None, :] == wanted[:, None])
    return jnp.any(hits, axis=1).astype(jnp.float32)[:, None]


def local(block_states, dest_dev, dest_slot, neighbours, coarse_map):
    n_dev = lax.axis_size("dev")
    my_dev = lax.axis_index("dev")
    group_me = lax.axis_index("grp")
    cell_fields = block_states.shape[1]
    plane_cell_count = SIDE_LENGTH * SIDE_LENGTH
    wanted = jnp.arange(DEVICE_PATCHES, dtype=jnp.int32)
    mine_dev = lax.dynamic_slice_in_dim(dest_dev, my_dev * P_DEV, P_DEV)
    mine_slot = lax.dynamic_slice_in_dim(dest_slot, my_dev * P_DEV, P_DEV)
    retained_lines = (
        (mine_dev[None, :] == my_dev) & (mine_slot[None, :] == wanted[:, None])
    ).astype(jnp.float32)
    plan_dev = dest_dev.reshape(n_dev, P_DEV)
    plan_slot = dest_slot.reshape(n_dev, P_DEV)
    lower_all = neighbours[0]
    upper_all = neighbours[1]
    redistributed_blocks = selected_lines(retained_lines, block_states)
    for distance in range(1, DEVICE_PATCHES):
        target_dev = (my_dev + distance) % n_dev
        source_dev = (my_dev + n_dev - distance) % n_dev
        sending = (mine_dev == target_dev).astype(jnp.float32)[None, :]
        arrived = passed_along(selected_lines(sending, block_states), "dev", distance)
        redistributed_blocks = redistributed_blocks + selected_lines(
            landing_rows(plan_dev, plan_slot, source_dev, my_dev, wanted), arrived
        )
    block_volumes = redistributed_blocks.reshape(
        DEVICE_PATCHES, cell_fields, SIDE_LENGTH, plane_cell_count
    )
    lower_nbr = lax.dynamic_slice_in_dim(lower_all, my_dev * DEVICE_PATCHES, DEVICE_PATCHES)
    upper_nbr = lax.dynamic_slice_in_dim(upper_all, my_dev * DEVICE_PATCHES, DEVICE_PATCHES)
    top_layers = block_volumes[:, :, SIDE_LENGTH - 2 :, :]
    bottom_layers = block_volumes[:, :, :2, :]
    empty = jnp.zeros((DEVICE_PATCHES, cell_fields, 2, plane_cell_count), jnp.float32)
    ghosts = add_faces(
        (empty, empty),
        (top_layers, bottom_layers),
        my_dev * DEVICE_PATCHES + wanted,
        lower_nbr,
        upper_nbr,
    )
    from_below = shifted((top_layers, bottom_layers), "dev", 1)
    labels_below = jnp.where(my_dev > 0, (my_dev - 1) * DEVICE_PATCHES + wanted, -3)
    ghosts = add_faces(ghosts, from_below, labels_below, lower_nbr, upper_nbr)
    from_above = shifted((top_layers, bottom_layers), "dev", -1)
    labels_above = jnp.where(my_dev < n_dev - 1, (my_dev + 1) * DEVICE_PATCHES + wanted, -3)
    ghosts = add_faces(ghosts, from_above, labels_above, lower_nbr, upper_nbr)
    lower_ghost, upper_ghost = ghosts
    lower_ghost, upper_ghost = fill_edges(
        block_volumes, lower_ghost, upper_ghost, lower_nbr, upper_nbr
    )
    advanced, interface = advance(block_volumes, lower_ghost, upper_ghost)
    out_state = advanced.reshape(DEVICE_PATCHES, cell_fields, SIDE_LENGTH**3)
    column = coarse_map[0]
    half_edge = SIDE_LENGTH // 2
    coarse = coarsen(interface).reshape(DEVICE_PATCHES, cell_fields * half_edge * half_edge)
    arrived = lax.all_gather(coarse, "grp", axis=0, tiled=True)
    matched = (column // DEVICE_PATCHES == group_me).astype(jnp.float32)
    placed = spread(
        arrived.reshape(arrived.shape[0], cell_fields, half_edge, half_edge),
        column % DEVICE_PATCHES,
    )
    registers = jnp.einsum("k,kfc->fc", matched, placed, precision=lax.Precision.HIGHEST)[None]
    return (out_state, registers)


def solution(mesh):
    in_specs = (P(("grp", "dev"), None, None), P("grp"), P("grp"), P(None, "grp"), P("dev", None))
    out_specs = (P(("grp", "dev"), None, None), P(("grp", "dev"), None, None))
    return jax.shard_map(local, mesh=mesh, in_specs=in_specs, out_specs=out_specs, check_vma=False)
```

profile of v0, /device:TPU:0, one launch (start us, length us, event | category | flops | bytes accessed | tf_op | source)
XLA Modules:
  0.0 61.7 jit_solution(8667873022805380065)
XLA Ops:
  0.7 0.7 %copy-done.1 = s32[32]{0:T(128)S(1)} copy-done((s32[32]{0:T(128)S(1)}, s32[32]{0:T(128)}, u32[]{:S(2)}) %copy-start.1) | copy-done | bytes 152
  1.5 0.3 copy-done
  1.7 0.4 fusion.2
  2.2 2.5 %collective-permute-start.2 = (f32[1,5,4096]{2,1,0:T(8,128)S(1)}, f32[1,5,4096]{2,1,0:T(8,128)S(1)}, u32[]{:S(2)}, u32[]{:S(2)}) collective-permute-start(f32[1,5,4096]{2,1,0:T(8,128)S(1)} %copy.68), channel_id=1, source_target_pairs={{1,0},{2,1},{3,2},{0,3},{5,4},{6,5},{7,6},{4,7},{9,8},{10,9},{11,1... | collective-permute-start | bytes 245768 | tf_op jit(solution)/shard_map/ppermute | solution.py:16
  4.7 0.4 fusion.4
  5.2 0.7 %collective-permute-start.1 = (f32[1,5,4096]{2,1,0:T(8,128)S(1)}, f32[1,5,4096]{2,1,0:T(8,128)S(1)}, u32[]{:S(2)}, u32[]{:S(2)}) collective-permute-start(f32[1,5,4096]{2,1,0:T(8,128)S(1)} %copy.67), channel_id=1, source_target_pairs={{2,0},{3,1},{0,2},{1,3},{6,4},{7,5},{4,6},{5,7},{10,8},{11,9},{8,1... | collective-permute-start | bytes 245768 | tf_op jit(solution)/shard_map/ppermute | solution.py:16
  5.8 0.4 fusion.6
  6.3 0.3 collective-permute-start
  6.6 0.1 reshape.337
  6.7 0.6 copy-done.4
  7.2 0.1 reshape.338
  7.5 0.1 fusion.26
  7.6 0.1 fusion.22
  7.8 0.7 %copy-done.2 = s32[2,16]{1,0:T(2,128)S(1)} copy-done((s32[2,16]{1,0:T(2,128)S(1)}, s32[2,16]{1,0:T(2,128)}, u32[]{:S(2)}) %copy-start.2) | copy-done | bytes 152
  8.4 0.1 broadcast_compare_fusion.2
  8.6 0.6 copy-done.3
  9.4 2.7 %collective-permute-done.1 = f32[1,5,4096]{2,1,0:T(8,128)S(1)} collective-permute-done((f32[1,5,4096]{2,1,0:T(8,128)S(1)}, f32[1,5,4096]{2,1,0:T(8,128)S(1)}, u32[]{:S(2)}, u32[]{:S(2)}) %collective-permute-start.1) | collective-permute-done | bytes 81952 | tf_op jit(solution)/shard_map/ppermute | solution.py:16
  12.1 0.4 collective-permute-done
  12.4 0.5 multiply_add_fusion
  12.9 0.2 reshape.339
  13.3 1.3 %collective-permute-start.5 = (f32[4,5,2,256]{3,2,1,0:T(2,128)S(1)}, f32[4,5,2,256]{3,2,1,0:T(2,128)S(1)}, u32[]{:S(2)}, u32[]{:S(2)}) collective-permute-start(f32[4,5,2,256]{3,2,1,0:T(2,128)S(1)} %copy.77), channel_id=1, source_target_pairs={{0,1},{1,2},{2,3},{4,5},{5,6},{6,7},{8,9},{9,10},{10,11},{12,13},{... | collective-permute-start | bytes 122888 | tf_op jit(solution)/shard_map/ppermute | solution.py:22
  14.6 1.3 %collective-permute-start.6 = (f32[4,5,2,256]{3,2,1,0:T(2,128)S(1)}, f32[4,5,2,256]{3,2,1,0:T(2,128)S(1)}, u32[]{:S(2)}, u32[]{:S(2)}) collective-permute-start(f32[4,5,2,256]{3,2,1,0:T(2,128)S(1)} %copy.77), channel_id=1, source_target_pairs={{1,0},{2,1},{3,2},{5,4},{6,5},{7,6},{9,8},{10,9},{11,10},{13,12},{... | collective-permute-start | bytes 122888 | tf_op jit(solution)/shard_map/ppermute | solution.py:22
  15.9 4.7 %collective-permute-start.3 = (f32[4,5,2,256]{3,2,1,0:T(2,128)S(1)}, f32[4,5,2,256]{3,2,1,0:T(2,128)S(1)}, u32[]{:S(2)}, u32[]{:S(2)}) collective-permute-start(f32[4,5,2,256]{3,2,1,0:T(2,128)S(1)} %copy.76), channel_id=1, source_target_pairs={{0,1},{1,2},{2,3},{4,5},{5,6},{6,7},{8,9},{9,10},{10,11},{12,13},{... | collective-permute-start | bytes 122888 | tf_op jit(solution)/shard_map/ppermute | solution.py:22
  20.7 1.3 %collective-permute-start.4 = (f32[4,5,2,256]{3,2,1,0:T(2,128)S(1)}, f32[4,5,2,256]{3,2,1,0:T(2,128)S(1)}, u32[]{:S(2)}, u32[]{:S(2)}) collective-permute-start(f32[4,5,2,256]{3,2,1,0:T(2,128)S(1)} %copy.76), channel_id=1, source_target_pairs={{1,0},{2,1},{3,2},{5,4},{6,5},{7,6},{9,8},{10,9},{11,10},{13,12},{... | collective-permute-start | bytes 122888 | tf_op jit(solution)/shard_map/ppermute | solution.py:22
  22.0 0.2 fusion.31
  22.2 0.2 fusion.35
  22.5 0.2 convolution_add_fusion.1
  22.8 0.2 fusion
  23.1 0.2 convolution_add_fusion.3
  23.3 1.7 %collective-permute-done.4 = f32[4,5,2,256]{3,2,1,0:T(2,128)S(1)} collective-permute-done((f32[4,5,2,256]{3,2,1,0:T(2,128)S(1)}, f32[4,5,2,256]{3,2,1,0:T(2,128)S(1)}, u32[]{:S(2)}, u32[]{:S(2)}) %collective-permute-start.4) | collective-permute-done | bytes 40992 | tf_op jit(solution)/shard_map/ppermute | solution.py:22
  25.1 0.2 fusion.1
  25.3 0.1 pad_maximum_fusion
  25.6 0.1 fusion.13
  25.7 0.4 slice_add_fusion
  26.0 0.1 slice_subtract_fusion.3
  26.5 0.2 multiply_bitcast_fusion
  26.7 0.1 multiply_dynamic-update-slice_fusion.4
  26.9 0.2 multiply_subtract_fusion
  27.1 0.8 %fusion.11 = f32[4,5,16,256]{3,0,2,1:T(4,128)} fusion(f32[4,5,16,256]{3,0,2,1:T(4,128)S(1)} %bitcast.134, f32[4,5,17,256]{3,0,2,1:T(4,128)S(1)} %multiply_subtract_fusion), kind=kLoop, calls=%fused_computation.21 | loop fusion | flops 245760 | bytes 1310720 | tf_op jit(solution)/shard_map/sub | solution.py:82
  27.9 0.2 copy.63
  28.2 0.4 reduce_sum.9
  28.6 0.3 copy.64
  28.9 0.1 reshape.347
  29.0 31.1 %all-gather = f32[8,4,320]{2,1,0:T(4,128)S(1)} all-gather(f32[1,4,320]{2,1,0:T(4,128)S(1)} %reshape.347), channel_id=1, replica_groups=mesh['grp'=8,'dev'=4] {'grp'}, dimensions={0}, use_global_device_ids=true | all-gather | bytes 46080 | tf_op jit(solution)/shard_map/all_gather | solution.py:192
  60.1 0.2 tile.8
  60.4 0.2 copy.65
  60.7 0.4 fusion.27
  61.1 0.6 %broadcast_in_dim.19 = f32[1,5,256]{2,0,1:T(1,128)} reshape(f32[5,256]{1,0:T(8,128)S(1)} %bitcast.147) | data formatting | bytes 10240 | tf_op jit(solution)/shard_map/broadcast_in_dim | solution.py:198
  (60 shorter events, 1.5 us)
Async XLA Ops:
  0.6 1.1 %copy-start = (f32[8,5,4096]{2,0,1:T(8,128)S(1)}, f32[8,5,4096]{2,0,1:T(8,128)}, u32[]{:S(2)}) copy-start(f32[8,5,4096]{2,0,1:T(8,128)} %param.5) | copy-start | bytes 1966084
  0.7 0.7 %copy-start.1 = (s32[32]{0:T(128)S(1)}, s32[32]{0:T(128)}, u32[]{:S(2)}) copy-start(s32[32]{0:T(128)} %param.6) | copy-start | bytes 388
  2.2 7.1 %collective-permute-start.2 = (f32[1,5,4096]{2,1,0:T(8,128)S(1)}, f32[1,5,4096]{2,1,0:T(8,128)S(1)}, u32[]{:S(2)}, u32[]{:S(2)}) collective-permute-start(f32[1,5,4096]{2,1,0:T(8,128)S(1)} %copy.68), channel_id=1, source_target_pairs={{1,0},{2,1},{3,2},{0,3},{5,4},{6,5},{7,6},{4,7},{9,8},{10,9},{11,1... | collective-permute-start | bytes 245768 | tf_op jit(solution)/shard_map/ppermute | solution.py:16
  5.2 6.9 %collective-permute-start.1 = (f32[1,5,4096]{2,1,0:T(8,128)S(1)}, f32[1,5,4096]{2,1,0:T(8,128)S(1)}, u32[]{:S(2)}, u32[]{:S(2)}) collective-permute-start(f32[1,5,4096]{2,1,0:T(8,128)S(1)} %copy.67), channel_id=1, source_target_pairs={{2,0},{3,1},{0,2},{1,3},{6,4},{7,5},{4,6},{5,7},{10,8},{11,9},{8,1... | collective-permute-start | bytes 245768 | tf_op jit(solution)/shard_map/ppermute | solution.py:16
  6.3 6.1 %collective-permute-start = (f32[1,5,4096]{2,1,0:T(8,128)S(1)}, f32[1,5,4096]{2,1,0:T(8,128)S(1)}, u32[]{:S(2)}, u32[]{:S(2)}) collective-permute-start(f32[1,5,4096]{2,1,0:T(8,128)S(1)} %copy.66), channel_id=1, source_target_pairs={{3,0},{0,1},{1,2},{2,3},{7,4},{4,5},{5,6},{6,7},{11,8},{8,9},{9,10... | collective-permute-start | bytes 245768 | tf_op jit(solution)/shard_map/ppermute | solution.py:16
  6.6 0.7 %copy-start.4 = (s32[32]{0:T(128)S(1)}, s32[32]{0:T(128)}, u32[]{:S(2)}) copy-start(s32[32]{0:T(128)} %param.7) | copy-start | bytes 388
  7.8 0.7 %copy-start.2 = (s32[2,16]{1,0:T(2,128)S(1)}, s32[2,16]{1,0:T(2,128)}, u32[]{:S(2)}) copy-start(s32[2,16]{1,0:T(2,128)} %param.8) | copy-start | bytes 388
  8.5 0.7 %copy-start.3 = (s32[1,32]{1,0:T(1,128)S(1)}, s32[1,32]{1,0:T(1,128)}, u32[]{:S(2)}) copy-start(s32[1,32]{1,0:T(1,128)} %param.9) | copy-start | bytes 388
  13.3 9.2 %collective-permute-start.5 = (f32[4,5,2,256]{3,2,1,0:T(2,128)S(1)}, f32[4,5,2,256]{3,2,1,0:T(2,128)S(1)}, u32[]{:S(2)}, u32[]{:S(2)}) collective-permute-start(f32[4,5,2,256]{3,2,1,0:T(2,128)S(1)} %copy.77), channel_id=1, source_target_pairs={{0,1},{1,2},{2,3},{4,5},{5,6},{6,7},{8,9},{9,10},{10,11},{12,13},{... | collective-permute-start | bytes 122888 | tf_op jit(solution)/shard_map/ppermute | solution.py:22
  14.6 8.2 %collective-permute-start.6 = (f32[4,5,2,256]{3,2,1,0:T(2,128)S(1)}, f32[4,5,2,256]{3,2,1,0:T(2,128)S(1)}, u32[]{:S(2)}, u32[]{:S(2)}) collective-permute-start(f32[4,5,2,256]{3,2,1,0:T(2,128)S(1)} %copy.77), channel_id=1, source_target_pairs={{1,0},{2,1},{3,2},{5,4},{6,5},{7,6},{9,8},{10,9},{11,10},{13,12},{... | collective-permute-start | bytes 122888 | tf_op jit(solution)/shard_map/ppermute | solution.py:22
  15.9 7.1 %collective-permute-start.3 = (f32[4,5,2,256]{3,2,1,0:T(2,128)S(1)}, f32[4,5,2,256]{3,2,1,0:T(2,128)S(1)}, u32[]{:S(2)}, u32[]{:S(2)}) collective-permute-start(f32[4,5,2,256]{3,2,1,0:T(2,128)S(1)} %copy.76), channel_id=1, source_target_pairs={{0,1},{1,2},{2,3},{4,5},{5,6},{6,7},{8,9},{9,10},{10,11},{12,13},{... | collective-permute-start | bytes 122888 | tf_op jit(solution)/shard_map/ppermute | solution.py:22
  20.7 4.4 %collective-permute-start.4 = (f32[4,5,2,256]{3,2,1,0:T(2,128)S(1)}, f32[4,5,2,256]{3,2,1,0:T(2,128)S(1)}, u32[]{:S(2)}, u32[]{:S(2)}) collective-permute-start(f32[4,5,2,256]{3,2,1,0:T(2,128)S(1)} %copy.76), channel_id=1, source_target_pairs={{1,0},{2,1},{3,2},{5,4},{6,5},{7,6},{9,8},{10,9},{11,10},{13,12},{... | collective-permute-start | bytes 122888 | tf_op jit(solution)/shard_map/ppermute | solution.py:22
where the time goes:
time: 62 us; the launch traced here: 61.7 us
  blocking collectives  31.1 us (50%)
  starting transfers between devices  12 us (19%)
  local copies, waits for them, and re-layouts  5.52 us (9%)
  waiting for transfers between devices  4.78 us (8%)
  other arithmetic  3.65 us (6%)
  matrix products  3.52 us (6%)
  between operations  1.14 us (2%)
    all_gather x1, blocking collectives, local(): arrived = lax.all_gather(coarse, 'grp', axis=0, tiled=True)  31.1 us
    ppermute x4, starting transfers between devices, shifted(): return lax.ppermute(shard, axis, pairs)  8.6 us
    ppermute x3, starting transfers between devices, passed_along(): return lax.ppermute(block, axis, route)  3.39 us
    dot_general x10, matrix products, selected_lines(): picked = jnp.dot(weights, flat, precision=lax.Precision.HIGHEST)  3.09 us
    ppermute x3, waiting for transfers between devices, passed_along(): return lax.ppermute(block, axis, route)  3.08 us
    unnamed x16, local copies, waits for them, and re-layouts  2.97 us
    ppermute x4, waiting for transfers between devices, shifted(): return lax.ppermute(shard, axis, pairs)  1.69 us
  transfers between devices with their start and end apart: 7, of which 3 were waited for; matrix products, arithmetic and copies ran while one was open for 5% of the time, Pallas kernels for 0%

commit v1 on v0

--- a/solution.py
+++ b/solution.py
@@ -8,6 +8,22 @@
 P_DEV = 8
 GAMMA = 1.4
 COURANT = 0.2
+
+
+def collect(x, axis, dim):
+    ways, here, step = (lax.axis_size(axis), lax.axis_index(axis), x.shape[dim])
+    shape = [n * ways if d == dim else n for d, n in enumerate(x.shape)]
+    full = lax.dynamic_update_slice_in_dim(jnp.zeros(shape, x.dtype), x, here * step, axis=dim)
+    going_up = going_down = x
+    for far in range(1, ways // 2 + 1):
+        going_up = lax.ppermute(going_up, axis, [(d, (d + 1) % ways) for d in range(ways)])
+        full = lax.dynamic_update_slice_in_dim(full, going_up, (here - far) % ways * step, axis=dim)
+        if 2 * far < ways:
+            going_down = lax.ppermute(going_down, axis, [(d, (d - 1) % ways) for d in range(ways)])
+            full = lax.dynamic_update_slice_in_dim(
+                full, going_down, (here + far) % ways * step, axis=dim
+            )
+    return full
 
 
 def passed_along(block, axis, distance):
@@ -189,7 +205,7 @@
     column = coarse_map[0]
     half_edge = SIDE_LENGTH // 2
     coarse = coarsen(interface).reshape(DEVICE_PATCHES, cell_fields * half_edge * half_edge)
-    arrived = lax.all_gather(coarse, "grp", axis=0, tiled=True)
+    arrived = collect(coarse, "grp", 0)
     matched = (column // DEVICE_PATCHES == group_me).astype(jnp.float32)
     placed = spread(
         arrived.reshape(arrived.shape[0], cell_fields, half_edge, half_edge),

time: 62 us -> 58.7 us (0.947)
  blocking collectives: 31.1 us -> 0 us
  starting transfers between devices: 12 us -> 26.4 us
  local copies, waits for them, and re-layouts: 5.52 us -> 14.2 us
  waiting for transfers between devices: 4.78 us -> 9.42 us
    all_gather x1 -> x0, blocking collectives: 31.1 us -> none  [local(): arrived = lax.all_gather(coarse, 'grp', axis=0, tiled=True)]
    ppermute x0 -> x7, starting transfers between devices: none -> 14.4 us  [the longest x3 12.8 us: collect(): lax.ppermute(going_down, axis, [(d, (d - 1) % ways) for d in range(ways)])]
    dynamic_update_slice x0 -> x8, local copies, waits for them, and re-layouts: none -> 8.05 us  [the longest x4 4.17 us: collect(): lax.dynamic_update_slice_in_dim(full, going_up, (here - far) % ways * ste...]
    ppermute x0 -> x7, waiting for transfers between devices: none -> 4.54 us  [the longest x4 4.53 us: collect(): lax.ppermute(going_up, axis, [(d, (d + 1) % ways) for d in range(ways)])]
    ppermute x0 -> x7, local copies, waits for them, and re-layouts: none -> 0.95 us  [the longest x4 0.55 us: collect(): lax.ppermute(going_up, axis, [(d, (d + 1) % ways) for d in range(ways)])]
    unnamed x16 -> x15, local copies, waits for them, and re-layouts: 2.97 us -> 2.88 us
  transfers between devices with their start and end apart: 7 -> 14, of which waited for: 3 -> 6; matrix products, arithmetic and copies ran while one was open for 5% -> 20% of each run, Pallas kernels for 0% -> 0%
where the time goes in v1:
time: 58.7 us; the launch traced here: 58.5 us
  starting transfers between devices  26.4 us (45%)
  local copies, waits for them, and re-layouts  14.2 us (24%)
  waiting for transfers between devices  9.42 us (16%)
  other arithmetic  3.63 us (6%)
  matrix products  3.52 us (6%)
  between operations  1.32 us (2%)
    ppermute x3, starting transfers between devices, collect(): lax.ppermute(going_down, axis, [(d, (d - 1) % ways) for d in range(ways)])  12.8 us
    ppermute x4, starting transfers between devices, shifted(): return lax.ppermute(shard, axis, pairs)  8.6 us
    ppermute x4, waiting for transfers between devices, collect(): lax.ppermute(going_up, axis, [(d, (d + 1) % ways) for d in range(ways)])  4.53 us
    dynamic_update_slice x4, local copies, waits for them, and re-layouts, collect(): lax.dynamic_update_slice_in_dim(full, going_up, (here - far) % ways * ste...  4.17 us
    ppermute x3, starting transfers between devices, passed_along(): return lax.ppermute(block, axis, route)  3.39 us
    ppermute x3, waiting for transfers between devices, passed_along(): return lax.ppermute(block, axis, route)  3.19 us
    dynamic_update_slice x3, local copies, waits for them, and re-layouts, collect(): lax.dynamic_update_slice_in_dim(full, going_down, (here + far) % ways * s...  3.12 us
    dot_general x10, matrix products, selected_lines(): picked = jnp.dot(weights, flat, precision=lax.Precision.HIGHEST)  3.09 us
  transfers between devices with their start and end apart: 14, of which 6 were waited for; matrix products, arithmetic and copies ran while one was open for 20% of the time, Pallas kernels for 0%

profile of v1, /device:TPU:0, one launch (start us, length us, event | category | flops | bytes accessed | tf_op | source)
XLA Modules:
  0.0 58.5 jit_solution(16362177235141520963)
XLA Ops:
  0.7 0.7 %copy-done.1 = s32[32]{0:T(128)S(1)} copy-done((s32[32]{0:T(128)S(1)}, s32[32]{0:T(128)}, u32[]{:S(2)}) %copy-start.1) | copy-done | bytes 152
  1.5 0.3 copy-done
  1.7 0.4 fusion.2
  2.2 2.5 %collective-permute-start.2 = (f32[1,5,4096]{2,1,0:T(8,128)S(1)}, f32[1,5,4096]{2,1,0:T(8,128)S(1)}, u32[]{:S(2)}, u32[]{:S(2)}) collective-permute-start(f32[1,5,4096]{2,1,0:T(8,128)S(1)} %copy.86), channel_id=1, source_target_pairs={{1,0},{2,1},{3,2},{0,3},{5,4},{6,5},{7,6},{4,7},{9,8},{10,9},{11,1... | collective-permute-start | bytes 245768 | tf_op jit(solution)/shard_map/ppermute | solution.py:32
  4.7 0.4 fusion.4
  5.2 0.7 %collective-permute-start.1 = (f32[1,5,4096]{2,1,0:T(8,128)S(1)}, f32[1,5,4096]{2,1,0:T(8,128)S(1)}, u32[]{:S(2)}, u32[]{:S(2)}) collective-permute-start(f32[1,5,4096]{2,1,0:T(8,128)S(1)} %copy.85), channel_id=1, source_target_pairs={{2,0},{3,1},{0,2},{1,3},{6,4},{7,5},{4,6},{5,7},{10,8},{11,9},{8,1... | collective-permute-start | bytes 245768 | tf_op jit(solution)/shard_map/ppermute | solution.py:32
  5.8 0.4 fusion.6
  6.3 0.3 collective-permute-start
  6.7 0.6 copy-done.4
  7.8 0.7 %copy-done.2 = s32[2,16]{1,0:T(2,128)S(1)} copy-done((s32[2,16]{1,0:T(2,128)S(1)}, s32[2,16]{1,0:T(2,128)}, u32[]{:S(2)}) %copy-start.2) | copy-done | bytes 152
  8.6 0.6 copy-done.3
  9.2 2.8 %collective-permute-done.1 = f32[1,5,4096]{2,1,0:T(8,128)S(1)} collective-permute-done((f32[1,5,4096]{2,1,0:T(8,128)S(1)}, f32[1,5,4096]{2,1,0:T(8,128)S(1)}, u32[]{:S(2)}, u32[]{:S(2)}) %collective-permute-start.1) | collective-permute-done | bytes 81952 | tf_op jit(solution)/shard_map/ppermute | solution.py:32
  12.1 0.4 collective-permute-done
  12.4 0.5 multiply_add_fusion
  12.9 0.2 reshape.339
  13.3 1.3 %collective-permute-start.5 = (f32[4,5,2,256]{3,2,1,0:T(2,128)S(1)}, f32[4,5,2,256]{3,2,1,0:T(2,128)S(1)}, u32[]{:S(2)}, u32[]{:S(2)}) collective-permute-start(f32[4,5,2,256]{3,2,1,0:T(2,128)S(1)} %copy.95), channel_id=1, source_target_pairs={{0,1},{1,2},{2,3},{4,5},{5,6},{6,7},{8,9},{9,10},{10,11},{12,13},{... | collective-permute-start | bytes 122888 | tf_op jit(solution)/shard_map/ppermute | solution.py:38
  14.6 1.3 %collective-permute-start.6 = (f32[4,5,2,256]{3,2,1,0:T(2,128)S(1)}, f32[4,5,2,256]{3,2,1,0:T(2,128)S(1)}, u32[]{:S(2)}, u32[]{:S(2)}) collective-permute-start(f32[4,5,2,256]{3,2,1,0:T(2,128)S(1)} %copy.95), channel_id=1, source_target_pairs={{1,0},{2,1},{3,2},{5,4},{6,5},{7,6},{9,8},{10,9},{11,10},{13,12},{... | collective-permute-start | bytes 122888 | tf_op jit(solution)/shard_map/ppermute | solution.py:38
  15.9 4.7 %collective-permute-start.3 = (f32[4,5,2,256]{3,2,1,0:T(2,128)S(1)}, f32[4,5,2,256]{3,2,1,0:T(2,128)S(1)}, u32[]{:S(2)}, u32[]{:S(2)}) collective-permute-start(f32[4,5,2,256]{3,2,1,0:T(2,128)S(1)} %copy.94), channel_id=1, source_target_pairs={{0,1},{1,2},{2,3},{4,5},{5,6},{6,7},{8,9},{9,10},{10,11},{12,13},{... | collective-permute-start | bytes 122888 | tf_op jit(solution)/shard_map/ppermute | solution.py:38
  20.7 1.3 %collective-permute-start.4 = (f32[4,5,2,256]{3,2,1,0:T(2,128)S(1)}, f32[4,5,2,256]{3,2,1,0:T(2,128)S(1)}, u32[]{:S(2)}, u32[]{:S(2)}) collective-permute-start(f32[4,5,2,256]{3,2,1,0:T(2,128)S(1)} %copy.94), channel_id=1, source_target_pairs={{1,0},{2,1},{3,2},{5,4},{6,5},{7,6},{9,8},{10,9},{11,10},{13,12},{... | collective-permute-start | bytes 122888 | tf_op jit(solution)/shard_map/ppermute | solution.py:38
  22.0 0.2 fusion.31
  22.2 0.2 fusion.35
  22.5 0.2 convolution_add_fusion.1
  22.8 0.2 fusion
  23.1 0.2 convolution_add_fusion.3
  23.3 1.7 %collective-permute-done.4 = f32[4,5,2,256]{3,2,1,0:T(2,128)S(1)} collective-permute-done((f32[4,5,2,256]{3,2,1,0:T(2,128)S(1)}, f32[4,5,2,256]{3,2,1,0:T(2,128)S(1)}, u32[]{:S(2)}, u32[]{:S(2)}) %collective-permute-start.4) | collective-permute-done | bytes 40992 | tf_op jit(solution)/shard_map/ppermute | solution.py:38
  25.1 0.2 fusion.1
  25.7 0.4 slice_add_fusion
  27.1 0.2 copy.74
  27.3 0.4 reduce_sum.9
  27.8 0.3 copy.75
  28.1 1.5 %collective-permute-start.7 = (f32[4,320]{1,0:T(4,128)S(1)}, f32[4,320]{1,0:T(4,128)S(1)}, u32[]{:S(2)}, u32[]{:S(2)}) collective-permute-start(f32[4,320]{1,0:T(4,128)S(1)} %div.74), channel_id=1, source_target_pairs={{0,4},{4,8},{8,12},{12,16},{16,20},{20,24},{24,28},{28,0},{1,5},{5... | collective-permute-start | bytes 15368 | tf_op jit(solution)/shard_map/ppermute | solution.py:19
  29.8 3.2 %collective-permute-start.8 = (f32[4,320]{1,0:T(4,128)S(1)}, f32[4,320]{1,0:T(4,128)S(1)}, u32[]{:S(2)}, u32[]{:S(2)}) collective-permute-start(f32[4,320]{1,0:T(4,128)S(1)} %div.74), channel_id=1, source_target_pairs={{0,28},{4,0},{8,4},{12,8},{16,12},{20,16},{24,20},{28,24},{1,29},{... | collective-permute-start | bytes 15368 | tf_op jit(solution)/shard_map/ppermute | solution.py:22
  33.0 1.5 %collective-permute-done.7 = f32[4,320]{1,0:T(4,128)S(1)} collective-permute-done((f32[4,320]{1,0:T(4,128)S(1)}, f32[4,320]{1,0:T(4,128)S(1)}, u32[]{:S(2)}, u32[]{:S(2)}) %collective-permute-start.7) | collective-permute-done | bytes 5152 | tf_op jit(solution)/shard_map/ppermute | solution.py:19
  34.6 4.8 %collective-permute-start.10 = (f32[4,320]{1,0:T(4,128)S(1)}, f32[4,320]{1,0:T(4,128)S(1)}, u32[]{:S(2)}, u32[]{:S(2)}) collective-permute-start(f32[4,320]{1,0:T(4,128)S(1)} %collective-permute-done.8), channel_id=1, source_target_pairs={{0,28},{4,0},{8,4},{12,8},{16,12},{20,16},{24,20},{28,24},{1,29},{... | collective-permute-start | bytes 15368 | tf_op jit(solution)/shard_map/ppermute | solution.py:22
  39.4 1.5 %collective-permute-done.9 = f32[4,320]{1,0:T(4,128)S(1)} collective-permute-done((f32[4,320]{1,0:T(4,128)S(1)}, f32[4,320]{1,0:T(4,128)S(1)}, u32[]{:S(2)}, u32[]{:S(2)}) %collective-permute-start.9) | collective-permute-done | bytes 5152 | tf_op jit(solution)/shard_map/ppermute | solution.py:19
  40.9 4.8 %collective-permute-start.12 = (f32[4,320]{1,0:T(4,128)S(1)}, f32[4,320]{1,0:T(4,128)S(1)}, u32[]{:S(2)}, u32[]{:S(2)}) collective-permute-start(f32[4,320]{1,0:T(4,128)S(1)} %collective-permute-done.10), channel_id=1, source_target_pairs={{0,28},{4,0},{8,4},{12,8},{16,12},{20,16},{24,20},{28,24},{1,29},{... | collective-permute-start | bytes 15368 | tf_op jit(solution)/shard_map/ppermute | solution.py:22
  45.7 1.5 %collective-permute-done.11 = f32[4,320]{1,0:T(4,128)S(1)} collective-permute-done((f32[4,320]{1,0:T(4,128)S(1)}, f32[4,320]{1,0:T(4,128)S(1)}, u32[]{:S(2)}, u32[]{:S(2)}) %collective-permute-start.11) | collective-permute-done | bytes 5152 | tf_op jit(solution)/shard_map/ppermute | solution.py:19
  47.2 0.8 %fusion.11 = f32[4,5,16,256]{3,0,2,1:T(4,128)} fusion(f32[4,5,16,256]{3,0,2,1:T(4,128)S(1)} %bitcast.135, f32[4,5,17,256]{3,0,2,1:T(4,128)S(1)} %multiply_subtract_fusion), kind=kLoop, calls=%fused_computation.21 | loop fusion | flops 245760 | bytes 1310720 | tf_op jit(solution)/shard_map/sub | solution.py:98
  48.2 0.8 %dynamic_update_slice.24 = f32[32,320]{0,1:T(8,128)S(1)} dynamic-update-slice(f32[32,320]{0,1:T(8,128)S(1)} %broadcast_in_dim.21, f32[4,320]{0,1:T(8,128)S(1)} %copy.76, s32[]{:T(128)S(6)} %select_n.188, s32[]{:T(128)} %constant.173.clone.1) | dynamic-update-slice | bytes 10244 | tf_op jit(solution)/shard_map/dynamic_update_slice | solution.py:16
  49.1 1.0 %dynamic_update_slice.25 = f32[32,320]{0,1:T(8,128)S(1)} dynamic-update-slice(f32[32,320]{0,1:T(8,128)S(1)} %dynamic_update_slice.24, f32[4,320]{0,1:T(8,128)S(1)} %copy.77, s32[]{:T(128)S(6)} %select_n.190, s32[]{:T(128)} %constant.173.clone.1) | dynamic-update-slice | bytes 10244 | tf_op jit(solution)/shard_map/dynamic_update_slice | solution.py:20
  50.3 1.0 %dynamic_update_slice.26 = f32[32,320]{0,1:T(8,128)S(1)} dynamic-update-slice(f32[32,320]{0,1:T(8,128)S(1)} %dynamic_update_slice.25, f32[4,320]{0,1:T(8,128)S(1)} %copy.78, s32[]{:T(128)S(6)} %select_n.192, s32[]{:T(128)} %constant.173.clone.1) | dynamic-update-slice | bytes 10244 | tf_op jit(solution)/shard_map/dynamic_update_slice | solution.py:23
  51.5 1.0 %dynamic_update_slice.27 = f32[32,320]{0,1:T(8,128)S(1)} dynamic-update-slice(f32[32,320]{0,1:T(8,128)S(1)} %dynamic_update_slice.26, f32[4,320]{0,1:T(8,128)S(1)} %copy.79, s32[]{:T(128)S(6)} %select_n.194, s32[]{:T(128)} %constant.173.clone.1) | dynamic-update-slice | bytes 10244 | tf_op jit(solution)/shard_map/dynamic_update_slice | solution.py:20
  52.7 1.0 %dynamic_update_slice.28 = f32[32,320]{0,1:T(8,128)S(1)} dynamic-update-slice(f32[32,320]{0,1:T(8,128)S(1)} %dynamic_update_slice.27, f32[4,320]{0,1:T(8,128)S(1)} %copy.80, s32[]{:T(128)S(6)} %select_n.196, s32[]{:T(128)} %constant.173.clone.1) | dynamic-update-slice | bytes 10244 | tf_op jit(solution)/shard_map/dynamic_update_slice | solution.py:23
  53.9 1.0 %dynamic_update_slice.29 = f32[32,320]{0,1:T(8,128)S(1)} dynamic-update-slice(f32[32,320]{0,1:T(8,128)S(1)} %dynamic_update_slice.28, f32[4,320]{0,1:T(8,128)S(1)} %copy.81, s32[]{:T(128)S(6)} %select_n.198, s32[]{:T(128)} %constant.173.clone.1) | dynamic-update-slice | bytes 10244 | tf_op jit(solution)/shard_map/dynamic_update_slice | solution.py:20
  55.1 1.0 %dynamic_update_slice.30 = f32[32,320]{0,1:T(8,128)S(1)} dynamic-update-slice(f32[32,320]{0,1:T(8,128)S(1)} %dynamic_update_slice.29, f32[4,320]{0,1:T(8,128)S(1)} %copy.82, s32[]{:T(128)S(6)} %select_n.200, s32[]{:T(128)} %constant.173.clone.1) | dynamic-update-slice | bytes 10244 | tf_op jit(solution)/shard_map/dynamic_update_slice | solution.py:23
  56.3 1.0 %dynamic_update_slice.31 = f32[32,320]{0,1:T(8,128)S(1)} dynamic-update-slice(f32[32,320]{0,1:T(8,128)S(1)} %dynamic_update_slice.30, f32[4,320]{0,1:T(8,128)S(1)} %copy.83, s32[]{:T(128)S(6)} %select_n.202, s32[]{:T(128)} %constant.173.clone.1) | dynamic-update-slice | bytes 10244 | tf_op jit(solution)/shard_map/dynamic_update_slice | solution.py:20
  57.4 0.4 fusion.27
  57.8 0.6 %broadcast_in_dim.22 = f32[1,5,256]{2,0,1:T(1,128)} reshape(f32[5,256]{1,0:T(8,128)S(1)} %bitcast.149) | data formatting | bytes 10240 | tf_op jit(solution)/shard_map/broadcast_in_dim | solution.py:214
  (88 shorter events, 4.0 us)
Async XLA Ops:
  0.6 1.1 %copy-start = (f32[8,5,4096]{2,0,1:T(8,128)S(1)}, f32[8,5,4096]{2,0,1:T(8,128)}, u32[]{:S(2)}) copy-start(f32[8,5,4096]{2,0,1:T(8,128)} %param.5) | copy-start | bytes 1966084
  0.7 0.7 %copy-start.1 = (s32[32]{0:T(128)S(1)}, s32[32]{0:T(128)}, u32[]{:S(2)}) copy-start(s32[32]{0:T(128)} %param.6) | copy-start | bytes 388
  2.2 7.0 %collective-permute-start.2 = (f32[1,5,4096]{2,1,0:T(8,128)S(1)}, f32[1,5,4096]{2,1,0:T(8,128)S(1)}, u32[]{:S(2)}, u32[]{:S(2)}) collective-permute-start(f32[1,5,4096]{2,1,0:T(8,128)S(1)} %copy.86), channel_id=1, source_target_pairs={{1,0},{2,1},{3,2},{0,3},{5,4},{6,5},{7,6},{4,7},{9,8},{10,9},{11,1... | collective-permute-start | bytes 245768 | tf_op jit(solution)/shard_map/ppermute | solution.py:32
  5.2 6.9 %collective-permute-start.1 = (f32[1,5,4096]{2,1,0:T(8,128)S(1)}, f32[1,5,4096]{2,1,0:T(8,128)S(1)}, u32[]{:S(2)}, u32[]{:S(2)}) collective-permute-start(f32[1,5,4096]{2,1,0:T(8,128)S(1)} %copy.85), channel_id=1, source_target_pairs={{2,0},{3,1},{0,2},{1,3},{6,4},{7,5},{4,6},{5,7},{10,8},{11,9},{8,1... | collective-permute-start | bytes 245768 | tf_op jit(solution)/shard_map/ppermute | solution.py:32
  6.3 6.1 %collective-permute-start = (f32[1,5,4096]{2,1,0:T(8,128)S(1)}, f32[1,5,4096]{2,1,0:T(8,128)S(1)}, u32[]{:S(2)}, u32[]{:S(2)}) collective-permute-start(f32[1,5,4096]{2,1,0:T(8,128)S(1)} %copy.84), channel_id=1, source_target_pairs={{3,0},{0,1},{1,2},{2,3},{7,4},{4,5},{5,6},{6,7},{11,8},{8,9},{9,10... | collective-permute-start | bytes 245768 | tf_op jit(solution)/shard_map/ppermute | solution.py:32
  6.6 0.7 %copy-start.4 = (s32[32]{0:T(128)S(1)}, s32[32]{0:T(128)}, u32[]{:S(2)}) copy-start(s32[32]{0:T(128)} %param.7) | copy-start | bytes 388
  7.8 0.7 %copy-start.2 = (s32[2,16]{1,0:T(2,128)S(1)}, s32[2,16]{1,0:T(2,128)}, u32[]{:S(2)}) copy-start(s32[2,16]{1,0:T(2,128)} %param.8) | copy-start | bytes 388
  8.5 0.7 %copy-start.3 = (s32[1,32]{1,0:T(1,128)S(1)}, s32[1,32]{1,0:T(1,128)}, u32[]{:S(2)}) copy-start(s32[1,32]{1,0:T(1,128)} %param.9) | copy-start | bytes 388
  13.3 9.2 %collective-permute-start.5 = (f32[4,5,2,256]{3,2,1,0:T(2,128)S(1)}, f32[4,5,2,256]{3,2,1,0:T(2,128)S(1)}, u32[]{:S(2)}, u32[]{:S(2)}) collective-permute-start(f32[4,5,2,256]{3,2,1,0:T(2,128)S(1)} %copy.95), channel_id=1, source_target_pairs={{0,1},{1,2},{2,3},{4,5},{5,6},{6,7},{8,9},{9,10},{10,11},{12,13},{... | collective-permute-start | bytes 122888 | tf_op jit(solution)/shard_map/ppermute | solution.py:38
  14.6 8.2 %collective-permute-start.6 = (f32[4,5,2,256]{3,2,1,0:T(2,128)S(1)}, f32[4,5,2,256]{3,2,1,0:T(2,128)S(1)}, u32[]{:S(2)}, u32[]{:S(2)}) collective-permute-start(f32[4,5,2,256]{3,2,1,0:T(2,128)S(1)} %copy.95), channel_id=1, source_target_pairs={{1,0},{2,1},{3,2},{5,4},{6,5},{7,6},{9,8},{10,9},{11,10},{13,12},{... | collective-permute-start | bytes 122888 | tf_op jit(solution)/shard_map/ppermute | solution.py:38
  15.9 7.1 %collective-permute-start.3 = (f32[4,5,2,256]{3,2,1,0:T(2,128)S(1)}, f32[4,5,2,256]{3,2,1,0:T(2,128)S(1)}, u32[]{:S(2)}, u32[]{:S(2)}) collective-permute-start(f32[4,5,2,256]{3,2,1,0:T(2,128)S(1)} %copy.94), channel_id=1, source_target_pairs={{0,1},{1,2},{2,3},{4,5},{5,6},{6,7},{8,9},{9,10},{10,11},{12,13},{... | collective-permute-start | bytes 122888 | tf_op jit(solution)/shard_map/ppermute | solution.py:38
  20.7 4.4 %collective-permute-start.4 = (f32[4,5,2,256]{3,2,1,0:T(2,128)S(1)}, f32[4,5,2,256]{3,2,1,0:T(2,128)S(1)}, u32[]{:S(2)}, u32[]{:S(2)}) collective-permute-start(f32[4,5,2,256]{3,2,1,0:T(2,128)S(1)} %copy.94), channel_id=1, source_target_pairs={{1,0},{2,1},{3,2},{5,4},{6,5},{7,6},{9,8},{10,9},{11,10},{13,12},{... | collective-permute-start | bytes 122888 | tf_op jit(solution)/shard_map/ppermute | solution.py:38
  28.1 6.4 %collective-permute-start.7 = (f32[4,320]{1,0:T(4,128)S(1)}, f32[4,320]{1,0:T(4,128)S(1)}, u32[]{:S(2)}, u32[]{:S(2)}) collective-permute-start(f32[4,320]{1,0:T(4,128)S(1)} %div.74), channel_id=1, source_target_pairs={{0,4},{4,8},{8,12},{12,16},{16,20},{20,24},{24,28},{28,0},{1,5},{5... | collective-permute-start | bytes 15368 | tf_op jit(solution)/shard_map/ppermute | solution.py:19
  29.8 4.8 %collective-permute-start.8 = (f32[4,320]{1,0:T(4,128)S(1)}, f32[4,320]{1,0:T(4,128)S(1)}, u32[]{:S(2)}, u32[]{:S(2)}) collective-permute-start(f32[4,320]{1,0:T(4,128)S(1)} %div.74), channel_id=1, source_target_pairs={{0,28},{4,0},{8,4},{12,8},{16,12},{20,16},{24,20},{28,24},{1,29},{... | collective-permute-start | bytes 15368 | tf_op jit(solution)/shard_map/ppermute | solution.py:22
  34.5 6.3 %collective-permute-start.9 = (f32[4,320]{1,0:T(4,128)S(1)}, f32[4,320]{1,0:T(4,128)S(1)}, u32[]{:S(2)}, u32[]{:S(2)}) collective-permute-start(f32[4,320]{1,0:T(4,128)S(1)} %collective-permute-done.7), channel_id=1, source_target_pairs={{0,4},{4,8},{8,12},{12,16},{16,20},{20,24},{24,28},{28,0},{1,5},{5... | collective-permute-start | bytes 15368 | tf_op jit(solution)/shard_map/ppermute | solution.py:19
  34.6 6.3 %collective-permute-start.10 = (f32[4,320]{1,0:T(4,128)S(1)}, f32[4,320]{1,0:T(4,128)S(1)}, u32[]{:S(2)}, u32[]{:S(2)}) collective-permute-start(f32[4,320]{1,0:T(4,128)S(1)} %collective-permute-done.8), channel_id=1, source_target_pairs={{0,28},{4,0},{8,4},{12,8},{16,12},{20,16},{24,20},{28,24},{1,29},{... | collective-permute-start | bytes 15368 | tf_op jit(solution)/shard_map/ppermute | solution.py:22
  40.9 6.3 %collective-permute-start.11 = (f32[4,320]{1,0:T(4,128)S(1)}, f32[4,320]{1,0:T(4,128)S(1)}, u32[]{:S(2)}, u32[]{:S(2)}) collective-permute-start(f32[4,320]{1,0:T(4,128)S(1)} %collective-permute-done.9), channel_id=1, source_target_pairs={{0,4},{4,8},{8,12},{12,16},{16,20},{20,24},{24,28},{28,0},{1,5},{5... | collective-permute-start | bytes 15368 | tf_op jit(solution)/shard_map/ppermute | solution.py:19
  40.9 14.1 %collective-permute-start.12 = (f32[4,320]{1,0:T(4,128)S(1)}, f32[4,320]{1,0:T(4,128)S(1)}, u32[]{:S(2)}, u32[]{:S(2)}) collective-permute-start(f32[4,320]{1,0:T(4,128)S(1)} %collective-permute-done.10), channel_id=1, source_target_pairs={{0,28},{4,0},{8,4},{12,8},{16,12},{20,16},{24,20},{28,24},{1,29},{... | collective-permute-start | bytes 15368 | tf_op jit(solution)/shard_map/ppermute | solution.py:22
  47.2 8.9 %collective-permute-start.13 = (f32[4,320]{1,0:T(4,128)S(1)}, f32[4,320]{1,0:T(4,128)S(1)}, u32[]{:S(2)}, u32[]{:S(2)}) collective-permute-start(f32[4,320]{1,0:T(4,128)S(1)} %collective-permute-done.11), channel_id=1, source_target_pairs={{0,4},{4,8},{8,12},{12,16},{16,20},{20,24},{24,28},{28,0},{1,5},{5... | collective-permute-start | bytes 15368 | tf_op jit(solution)/shard_map/ppermute | solution.py:19
